TPU v7x, 32 devices: a whole 2x2x4 slice. The times are simulated.
32 devices in a mesh: parts: 2 (over x), chol: 16 (over z, y, core).
Axes of the slice: x: 2, y: 2, z: 4, core: 2. Of those that a mesh axis runs over, the one named last changes fastest.
Arguments:
- orbitals: float32 [32, 100, 1024], P(('parts', 'chol')), parts along dimension 0, may hold values from -6 to 6
- intersection_inv: float32 [32, 100, 100], P(('parts', 'chol')), parts along dimension 0, may hold values from -0.625 to 0.625
- factor_rows: bfloat16 [4096, 1024], P('chol'), may hold values from -0.1875 to 0.1875
- factor_rotated: bfloat16 [100, 4096], replicated, may hold values from -0.625 to 0.625
- factor_core: bfloat16 [1024, 4096], P('chol'), may hold values from -0.125 to 0.125
- fields: float32 [32, 1024], P('parts', 'chol'), parts along dimension 0, may hold values from -6 to 6
Outputs:
- propagated: float32 [32, 100, 1024], P(('parts', 'chol')), parts along dimension 0
- force_bias: float32 [32, 1024], P('parts', 'chol'), parts along dimension 0
There are 2 independent parts, one for each index of `parts`. A program takes and returns all parts, laid end to end along the dimension named above; an argument that names none is the same for every part. Nothing has to cross between parts.
All inputs are finite; a program needn't handle non-finite values.
Results may differ from a plain program's by a relative error of at most 0.0091.
Values may be sent and summed in bfloat16 or wider, within the bound.
A program may use at most 64 MiB of HBM per device.

v0:
```python
import jax
import jax.numpy as jnp
from jax import lax
from jax.sharding import PartitionSpec as P

TAYLOR = 4


def density_one(half_green, all_rows, factor_rotated):
    projected = lax.dot_general(
        half_green, all_rows, (((1,), (1,)), ((), ())), preferred_element_type=jnp.float32
    )
    return jnp.sum(factor_rotated.astype(jnp.float32) * projected, axis=0).astype(jnp.bfloat16)


def propagate_one(orbital, potential, all_rows):
    total = orbital
    term = orbital
    for order in range(1, TAYLOR + 1):
        summed = lax.dot_general(
            term.astype(jnp.bfloat16),
            all_rows,
            (((1,), (1,)), ((), ())),
            preferred_element_type=jnp.float32,
        )
        scaled = (summed * potential[None, :] / order).astype(jnp.bfloat16)
        term = jnp.dot(scaled, all_rows, preferred_element_type=jnp.float32)
        total = total + term
    return total


def on_device(orbitals, intersection_inv, factor_rows, factor_rotated, factor_core, fields):
    walker_count = orbitals.shape[0]
    half_green = jnp.einsum(
        "wij,wjm->wim", intersection_inv, orbitals, precision=lax.Precision.HIGHEST
    ).astype(jnp.bfloat16)
    all_rows = lax.all_gather(factor_rows, "chol", axis=0, tiled=True)
    own_density = lax.map(lambda item: density_one(item, all_rows, factor_rotated), half_green)
    density = lax.all_gather(own_density, "chol", axis=0, tiled=True)
    force_bias = lax.dot_general(
        density, factor_core, (((1,), (1,)), ((), ())), preferred_element_type=jnp.float32
    )
    shifted = (fields - force_bias).astype(jnp.bfloat16)
    partial_sum = jnp.dot(shifted, factor_core, preferred_element_type=jnp.float32)
    summed_all = lax.psum(partial_sum, "chol")
    potential = lax.dynamic_slice_in_dim(
        summed_all, lax.axis_index("chol") * walker_count, walker_count, 0
    )
    propagated = lax.map(
        lambda pair: propagate_one(pair[0], pair[1], all_rows), (orbitals, potential)
    )
    return (propagated, force_bias)


def solution(mesh):
    in_specs = (
        P(("parts", "chol"), None, None),
        P(("parts", "chol"), None, None),
        P("chol", None),
        P(),
        P("chol", None),
        P("parts", "chol"),
    )
    out_specs = (P(("parts", "chol"), None, None), P("parts", "chol"))
    return jax.shard_map(
        on_device, mesh=mesh, in_specs=in_specs, out_specs=out_specs, check_vma=False
    )
```

profile of v0, /device:TPU:0, one launch (start us, length us, event | category | flops | bytes accessed | tf_op | source)
XLA Modules:
  0.0 249.2 jit_solution(8666170632495442712)
XLA Ops:
  7.2 0.0 copy-start
  7.2 0.0 copy-start.1
  7.2 0.0 copy-start.3
  7.2 0.0 all-gather.3.cloned.1.call-start
  7.2 0.7 all-gather.3.cloned.1.call-update
  7.9 0.0 all-reduce.2.cloned.1.call-start
  8.0 1.6 convolution_convert_fusion
  9.6 77.7 %all-gather.3.cloned.1.call-done = bf16[4096,1024]{1,0:T(8,128)(2,1)} async-done(((bf16[256,1024]{1,0:T(8,128)(2,1)}), bf16[4096,1024]{1,0:T(8,128)(2,1)}) %all-gather.3.cloned.1.call-update) | async-done | bytes 8388624 | tf_op jit(solution)/shard_map/all_gather | solution.py:37
  87.2 6.3 %fusion.7 = bf16[4096]{0:T(1024)(128)(2,1)S(1)} fusion(bf16[100,1024]{1,0:T(8,128)(2,1)S(1)} %convolution_convert_fusion, bf16[4096,1024]{1,0:T(8,128)(2,1)} %all-gather.3.cloned.1.call-done, bf16[100,4096]{1,0:T(8,128)(2,1)} %param.9), kind=kOutput, calls=%fused_computation.12 | convolution fusion | flops 840085504 | bytes 9420800 | tf_op jit(solution)/shard_map/while/body/eval_jaxpr/dot_general | solution.py:10
  93.5 19.5 %all-gather = bf16[65536]{0:T(1024)(128)(2,1)S(1)} all-gather(bf16[4096]{0:T(1024)(128)(2,1)S(1)} %fusion.7), channel_id=2, replica_groups=mesh['parts'=2,'chol'=16] {'chol'}, dimensions={0}, use_global_device_ids=true | all-gather | bytes 139264 | tf_op jit(solution)/shard_map/all_gather | solution.py:39
  113.0 0.1 reshape.20
  113.1 0.0 copy-done
  113.1 0.2 fusion.28
  113.3 0.0 copy-done.3
  113.3 0.0 copy-start.2
  113.3 0.9 fusion.24
  114.2 0.0 all-reduce.2.cloned.1.call-update
  114.3 87.1 %all-reduce.2.cloned.1.call-done = f32[16,4096]{1,0:T(8,128)} async-done(((f32[16,4096]{1,0:T(8,128)}), f32[16,4096]{1,0:T(8,128)}) %all-reduce.2.cloned.1.call-update) | async-done | bytes 262160 | tf_op jit(solution)/shard_map/psum | solution.py:45
  201.4 0.9 constant_dynamic-slice_fusion
  202.3 0.0 copy-done.1
  202.3 9.7 %fusion.11 = f32[100,1024]{1,0:T(8,128)S(1)} fusion(bf16[4096,1024]{1,0:T(8,128)(2,1)} %all-gather.3.cloned.1.call-done, f32[4096]{0:T(1024)S(1)} %bitcast.32, f32[1,100,1024]{2,0,1:T(1,128)S(1)} %copy-done.1), kind=kOutput, calls=%fused_computation.18 | convolution fusion | flops 1678540800 | bytes 9224192 | tf_op jit(solution)/shard_map/while/body/eval_jaxpr/dot_general | solution.py:27
  212.0 0.0 copy-done.2
  212.0 9.7 %fusion.10 = f32[100,1024]{1,0:T(8,128)S(1)} fusion(bf16[4096,1024]{1,0:T(8,128)(2,1)} %all-gather.3.cloned.1.call-done, f32[4096]{0:T(1024)S(1)} %bitcast.33, f32[100,1024]{1,0:T(8,128)S(1)} %fusion.11), kind=kOutput, calls=%fused_computation.17 | convolution fusion | flops 1679052800 | bytes 9224192 | tf_op jit(solution)/shard_map/while/body/eval_jaxpr/dot_general | solution.py:27
  221.7 9.7 %fusion.9 = f32[100,1024]{1,0:T(8,128)S(1)} fusion(bf16[4096,1024]{1,0:T(8,128)(2,1)} %all-gather.3.cloned.1.call-done, f32[4096]{0:T(1024)S(1)} %bitcast.34, f32[100,1024]{1,0:T(8,128)S(1)} %fusion.10), kind=kOutput, calls=%fused_computation.16 | convolution fusion | flops 1679052800 | bytes 9224192 | tf_op jit(solution)/shard_map/while/body/eval_jaxpr/dot_general | solution.py:27
  231.5 9.7 %fusion.8 = f32[1,100,1024]{2,1,0:T(8,128)S(1)} fusion(bf16[4096,1024]{1,0:T(8,128)(2,1)} %all-gather.3.cloned.1.call-done, f32[4096]{0:T(1024)S(1)} %bitcast.35, f32[100,1024]{1,0:T(8,128)S(1)} %fusion.9, f32[100,1024]{1,0:T(8,128)S(1)} %fusion.10, f32[100,1024]{1,0:T(8,128)S(1)} %fusion.11, f32[1,100,1024]{2,0,1:T(1,128)S(1)} %copy-done.1), kind=kOutput, calls=%fused_computation.14 | convolution fusion | flops 1679462400 | bytes 10452992 | tf_op jit(solution)/shard_map/while/body/eval_jaxpr/dot_general | solution.py:27
  241.2 1.2 copy.9
Async XLA Ops:
  7.2 105.9 %copy-start = (bf16[64,4096]{1,0:T(8,128)(2,1)S(1)}, bf16[64,4096]{1,0:T(8,128)(2,1)}, u32[]{:S(2)}) copy-start(bf16[64,4096]{1,0:T(8,128)(2,1)} %param.10) | copy-start | bytes 1572868
  7.2 195.2 %copy-start.1 = (f32[1,100,1024]{2,0,1:T(1,128)S(1)}, f32[1,100,1024]{2,0,1:T(1,128)}, u32[]{:S(2)}) copy-start(f32[1,100,1024]{2,0,1:T(1,128)} %param.6) | copy-start | bytes 1228804
  7.2 106.1 %copy-start.3 = (f32[16,64]{1,0:T(8,128)S(1)}, f32[16,64]{1,0:T(8,128)}, u32[]{:S(2)}) copy-start(f32[16,64]{1,0:T(8,128)} %param.11) | copy-start | bytes 12292
  7.2 80.0 %all-gather.3.cloned.1.call-start = ((), (), s32[]{:S(2)}) async-start(), calls=%async_computation | async-start | bytes 8912896 | tf_op jit(solution)/shard_map/all_gather | solution.py:37
  7.9 193.5 %all-reduce.2.cloned.1.call-start = ((), (), s32[]{:S(2)}) async-start(), calls=%async_computation.1 | async-start | bytes 524288 | tf_op jit(solution)/shard_map/psum | solution.py:45
  113.3 98.7 %copy-start.2 = (f32[16,64]{1,0:T(8,128)}, f32[16,64]{1,0:T(8,128)S(1)}, u32[]{:S(2)}) copy-start(f32[16,64]{1,0:T(8,128)S(1)} %fusion.28) | copy-start | bytes 12292
Sparse Core Ops, SparseCore 0:
  10.2 77.0 all-gather.2
  114.4 86.9 all-reduce.1
where the time goes:
time: 249 us
  waiting for transfers between devices  166 us (67%)
  matrix products  47.9 us (19%)
  blocking collectives  19.5 us (8%)
  between operations  14.1 us (6%)
    psum x1, waiting for transfers between devices, on_device(): summed_all = lax.psum(partial_sum, 'chol')  87.1 us
    all_gather x1, waiting for transfers between devices, on_device(): all_rows = lax.all_gather(factor_rows, 'chol', axis=0, tiled=True)  77.7 us
    dot_general x4, matrix products, propagate_one(): term = jnp.dot(scaled, all_rows, preferred_element_type=jnp.float32)  38.9 us
    all_gather x1, blocking collectives, on_device(): density = lax.all_gather(own_density, 'chol', axis=0, tiled=True)  19.5 us
    dot_general x1, matrix products, density_one(): lax.dot_general(half_green, all_rows, (((1,), (1,)), ((), ())), preferred...  6.26 us
  transfers between devices with their start and end apart: 2, of which 2 were waited for; matrix products, arithmetic and copies ran while one was open for 1% of the time, Pallas kernels for 0%

commit v1 on v0

--- a/solution.py
+++ b/solution.py
@@ -42,7 +42,12 @@
     )
     shifted = (fields - force_bias).astype(jnp.bfloat16)
     partial_sum = jnp.dot(shifted, factor_core, preferred_element_type=jnp.float32)
-    summed_all = lax.psum(partial_sum, "chol")
+
+    def _touch_plane(shard_in, named_axis):
+        raw_out = jnp.sum(lax.all_gather(shard_in, named_axis), axis=0)
+        return raw_out
+
+    summed_all = _touch_plane(partial_sum, "chol")
     potential = lax.dynamic_slice_in_dim(
         summed_all, lax.axis_index("chol") * walker_count, walker_count, 0
     )

time: 249 us -> 212 us (0.85)
  waiting for transfers between devices: 166 us -> 126 us
    psum x1 -> x0, waiting for transfers between devices: 87.1 us -> none  [on_device(): summed_all = lax.psum(partial_sum, 'chol')]
    all_gather x0 -> x1, waiting for transfers between devices: none -> 47.8 us  [_touch_plane(): raw_out = jnp.sum(lax.all_gather(shard_in, named_axis), axis=0)]
where the time goes in v1:
time: 212 us; the launch traced here: 211 us
  waiting for transfers between devices  126 us (59%)
  matrix products  47.9 us (23%)
  blocking collectives  19.5 us (9%)
  between operations  14.1 us (7%)
  other arithmetic  2.4 us (1%)
    all_gather x1, waiting for transfers between devices, on_device(): all_rows = lax.all_gather(factor_rows, 'chol', axis=0, tiled=True)  77.6 us
    all_gather x1, waiting for transfers between devices, _touch_plane(): raw_out = jnp.sum(lax.all_gather(shard_in, named_axis), axis=0)  47.8 us
    dot_general x4, matrix products, propagate_one(): term = jnp.dot(scaled, all_rows, preferred_element_type=jnp.float32)  38.8 us
    all_gather x1, blocking collectives, on_device(): density = lax.all_gather(own_density, 'chol', axis=0, tiled=True)  19.5 us
    dot_general x1, matrix products, density_one(): lax.dot_general(half_green, all_rows, (((1,), (1,)), ((), ())), preferred...  6.26 us
  transfers between devices with their start and end apart: 2, of which 2 were waited for; matrix products, arithmetic and copies ran while one was open for 1% of the time, Pallas kernels for 0%

profile of v1, /device:TPU:0, one launch (start us, length us, event | category | flops | bytes accessed | tf_op | source)
XLA Modules:
  0.0 211.3 jit_solution(13803351827885669895)
XLA Ops:
  7.2 0.0 copy-start
  7.2 0.0 copy-start.3
  7.2 0.0 all-gather.5.cloned.1.call-start
  7.2 0.7 all-gather.5.cloned.1.call-update
  7.9 0.0 copy-start.1
  7.9 0.0 all-gather.7.cloned.1.call-start
  8.0 1.6 convolution_convert_fusion
  9.6 77.6 %all-gather.5.cloned.1.call-done = bf16[4096,1024]{1,0:T(8,128)(2,1)} async-done(((bf16[256,1024]{1,0:T(8,128)(2,1)}), bf16[4096,1024]{1,0:T(8,128)(2,1)}) %all-gather.5.cloned.1.call-update) | async-done | bytes 8388624 | tf_op jit(solution)/shard_map/all_gather | solution.py:37
  87.2 6.3 %fusion.7 = bf16[4096]{0:T(1024)(128)(2,1)S(1)} fusion(bf16[100,1024]{1,0:T(8,128)(2,1)S(1)} %convolution_convert_fusion, bf16[4096,1024]{1,0:T(8,128)(2,1)} %all-gather.5.cloned.1.call-done, bf16[100,4096]{1,0:T(8,128)(2,1)} %param.9), kind=kOutput, calls=%fused_computation.12 | convolution fusion | flops 840085504 | bytes 9420800 | tf_op jit(solution)/shard_map/while/body/eval_jaxpr/dot_general | solution.py:10
  93.5 19.5 %all-gather = bf16[65536]{0:T(1024)(128)(2,1)S(1)} all-gather(bf16[4096]{0:T(1024)(128)(2,1)S(1)} %fusion.7), channel_id=2, replica_groups=mesh['parts'=2,'chol'=16] {'chol'}, dimensions={0}, use_global_device_ids=true | all-gather | bytes 139264 | tf_op jit(solution)/shard_map/all_gather | solution.py:39
  113.0 0.1 reshape.20
  113.1 0.0 copy-done
  113.1 0.2 fusion.28
  113.3 0.0 copy-done.3
  113.3 0.0 copy-start.2
  113.3 0.9 fusion.24
  114.2 0.0 all-gather.7.cloned.1.call-update
  114.3 47.8 %all-gather.7.cloned.1.call-done = f32[256,4096]{1,0:T(8,128)} async-done(((f32[16,4096]{1,0:T(8,128)}), f32[256,4096]{1,0:T(8,128)}) %all-gather.7.cloned.1.call-update) | async-done | bytes 4194320 | tf_op jit(solution)/shard_map/all_gather | solution.py:47
  162.0 2.4 %reduce_sum.20 = f32[16,4096]{1,0:T(8,128)S(1)} reduce(f32[16,16,4096]{2,1,0:T(8,128)} %bitcast.33, f32[]{:T(128)} %constant.24.clone.1), dimensions={0}, to_apply=%region_1.0 | reduce | flops 983040 | bytes 4456452 | tf_op jit(solution)/shard_map/reduce_sum | solution.py:47
  164.5 0.0 copy-done.1
  164.5 9.7 %fusion.11 = f32[100,1024]{1,0:T(8,128)S(1)} fusion(bf16[4096,1024]{1,0:T(8,128)(2,1)} %all-gather.5.cloned.1.call-done, f32[4096]{0:T(1024)S(1)} %bitcast.34, f32[1,100,1024]{2,0,1:T(1,128)S(1)} %copy-done.1), kind=kOutput, calls=%fused_computation.18 | convolution fusion | flops 1678540800 | bytes 9224192 | tf_op jit(solution)/shard_map/while/body/eval_jaxpr/dot_general | solution.py:27
  174.2 0.0 copy-done.2
  174.2 9.7 %fusion.10 = f32[100,1024]{1,0:T(8,128)S(1)} fusion(bf16[4096,1024]{1,0:T(8,128)(2,1)} %all-gather.5.cloned.1.call-done, f32[4096]{0:T(1024)S(1)} %bitcast.35, f32[100,1024]{1,0:T(8,128)S(1)} %fusion.11), kind=kOutput, calls=%fused_computation.17 | convolution fusion | flops 1679052800 | bytes 9224192 | tf_op jit(solution)/shard_map/while/body/eval_jaxpr/dot_general | solution.py:27
  183.8 9.7 %fusion.9 = f32[100,1024]{1,0:T(8,128)S(1)} fusion(bf16[4096,1024]{1,0:T(8,128)(2,1)} %all-gather.5.cloned.1.call-done, f32[4096]{0:T(1024)S(1)} %bitcast.36, f32[100,1024]{1,0:T(8,128)S(1)} %fusion.10), kind=kOutput, calls=%fused_computation.16 | convolution fusion | flops 1679052800 | bytes 9224192 | tf_op jit(solution)/shard_map/while/body/eval_jaxpr/dot_general | solution.py:27
  193.6 9.7 %fusion.8 = f32[1,100,1024]{2,1,0:T(8,128)S(1)} fusion(bf16[4096,1024]{1,0:T(8,128)(2,1)} %all-gather.5.cloned.1.call-done, f32[4096]{0:T(1024)S(1)} %bitcast.37, f32[100,1024]{1,0:T(8,128)S(1)} %fusion.9, f32[100,1024]{1,0:T(8,128)S(1)} %fusion.10, f32[100,1024]{1,0:T(8,128)S(1)} %fusion.11, f32[1,100,1024]{2,0,1:T(1,128)S(1)} %copy-done.1), kind=kOutput, calls=%fused_computation.14 | convolution fusion | flops 1679462400 | bytes 10452992 | tf_op jit(solution)/shard_map/while/body/eval_jaxpr/dot_general | solution.py:27
  203.3 1.2 copy.9
  (1 shorter events, 0.0 us)
Async XLA Ops:
  7.2 105.9 %copy-start = (bf16[64,4096]{1,0:T(8,128)(2,1)S(1)}, bf16[64,4096]{1,0:T(8,128)(2,1)}, u32[]{:S(2)}) copy-start(bf16[64,4096]{1,0:T(8,128)(2,1)} %param.10) | copy-start | bytes 1572868
  7.2 106.1 %copy-start.3 = (f32[16,64]{1,0:T(8,128)S(1)}, f32[16,64]{1,0:T(8,128)}, u32[]{:S(2)}) copy-start(f32[16,64]{1,0:T(8,128)} %param.11) | copy-start | bytes 12292
  7.2 80.0 %all-gather.5.cloned.1.call-start = ((), (), s32[]{:S(2)}) async-start(), calls=%async_computation | async-start | bytes 8912896 | tf_op jit(solution)/shard_map/all_gather | solution.py:37
  7.9 156.5 %copy-start.1 = (f32[1,100,1024]{2,0,1:T(1,128)S(1)}, f32[1,100,1024]{2,0,1:T(1,128)}, u32[]{:S(2)}) copy-start(f32[1,100,1024]{2,0,1:T(1,128)} %param.6) | copy-start | bytes 1228804
  7.9 154.1 %all-gather.7.cloned.1.call-start = ((), (), s32[]{:S(2)}) async-start(), calls=%async_computation.1 | async-start | bytes 4456448 | tf_op jit(solution)/shard_map/all_gather | solution.py:47
  113.3 60.8 %copy-start.2 = (f32[16,64]{1,0:T(8,128)}, f32[16,64]{1,0:T(8,128)S(1)}, u32[]{:S(2)}) copy-start(f32[16,64]{1,0:T(8,128)S(1)} %fusion.28) | copy-start | bytes 12292
Sparse Core Ops, SparseCore 0:
  10.2 77.0 all-gather.4
  114.4 47.5 all-gather.6
